TPU v7x, 128 devices: a whole 4x4x4 slice. The times are simulated.
128 devices in a mesh: role: 2 (over core), dev: 64 (over z, y, x).
Axes of the slice: x: 4, y: 4, z: 4, core: 2. Of those that a mesh axis runs over, the one named last changes fastest.
Arguments:
- moe_rows: bfloat16 [4096, 3584], P(('role', 'dev')), may hold values from -6 to 6
- expert_ids: int32 [4096, 8], P(('role', 'dev')), may hold values from 0 to 63, all different within a row; in each aligned block of 32 rows (0 to 31, 32 to 63, ...) at most 8 rows name the same one
- gate_weights: float32 [4096, 8], P(('role', 'dev')), may hold values from 0.05 to 0.6
- w_gate: bfloat16 [64, 3584, 1024], P('dev', None, 'role'), may hold values from -0.09375 to 0.09375
- w_up: bfloat16 [64, 3584, 1024], P('dev', None, 'role'), may hold values from -0.09375 to 0.09375
- w_down: bfloat16 [64, 3584, 1024], P('dev', None, 'role'), may hold values from -0.1875 to 0.1875
- q_latent: bfloat16 [512, 64, 512], P(('role', 'dev')), may hold values from -40 to 40
- q_rope: bfloat16 [512, 4096], P(('role', 'dev')), may hold values from -4 to 4
- latent_cache: bfloat16 [512, 2048, 512], P(('role', 'dev')), may hold values from -4 to 4
- rope_cache: bfloat16 [512, 64, 2048], P(('role', 'dev')), may hold values from -4 to 4
- lengths: int32 [512], P(('role', 'dev')), may hold values from 2 to 2048, as said below
Outputs:
- moe_out: bfloat16 [4096, 3584], P(('role', 'dev'))
- attended: bfloat16 [512, 64, 512], P(('role', 'dev'))
Inputs may be any that keep to these rules, and one draw needn't show every extreme that they name: `expert_ids`: each row names 8 different experts; among the rows of one device no expert is named more than 8 times. `lengths`: the first row holds all 2048 cached tokens.
All inputs are finite; a program needn't handle non-finite values.
Results may differ from a plain program's by a relative error of at most 0.0057.
Values may be sent and summed in bfloat16 or wider, within the bound.
A program may use at most 128 MiB of HBM per device.

v0:
```python
import jax
import jax.numpy as jnp
from jax import lax
from jax.sharding import PartitionSpec as P

score_scale = 192.0 ** (-0.5)


def expert_block(chosen, gate_matrix, up_matrix, down_matrix):
    gate_part = jnp.dot(chosen, gate_matrix, preferred_element_type=jnp.float32)
    up_part = jnp.dot(chosen, up_matrix, preferred_element_type=jnp.float32)
    hidden_units = (jax.nn.silu(gate_part) * up_part).astype(jnp.bfloat16)
    return lax.dot_general(
        hidden_units, down_matrix, (((1,), (1,)), ((), ())), preferred_element_type=jnp.float32
    )


def attend_row(query_lat, query_rope, cache_lat, cache_rope, length):
    head_count = query_lat.shape[0]
    rope_width = cache_rope.shape[0]
    scores = lax.dot_general(
        query_lat, cache_lat, (((1,), (1,)), ((), ())), preferred_element_type=jnp.float32
    )
    scores = scores + jnp.dot(
        query_rope.reshape(head_count, rope_width), cache_rope, preferred_element_type=jnp.float32
    )
    scores = scores * score_scale
    positions = jnp.arange(cache_lat.shape[0], dtype=jnp.int32)
    valid = (positions < length)[None, :]
    scores = jnp.where(valid, scores, jnp.float32(-1e30))
    highest = jnp.max(scores, axis=1, keepdims=True)
    weights = jnp.where(valid, jnp.exp(scores - highest), jnp.float32(0.0))
    probs = (weights / jnp.sum(weights, axis=1, keepdims=True)).astype(jnp.bfloat16)
    return jnp.dot(probs, cache_lat, preferred_element_type=jnp.float32).astype(jnp.bfloat16)


def per_device(
    moe_rows,
    expert_ids,
    gate_weights,
    w_gate,
    w_up,
    w_down,
    q_latent,
    q_rope,
    latent_cache,
    rope_cache,
    lengths,
):
    tok_count = moe_rows.shape[0]
    width = moe_rows.shape[1]
    topk_count = expert_ids.shape[1]
    experts = lax.axis_size("dev")
    capacity = min(tok_count, 2 * tok_count * topk_count // experts)
    flat_ids = expert_ids.reshape(-1)
    pair_count = flat_ids.shape[0]
    one_hot = (flat_ids[:, None] == jnp.arange(experts, dtype=jnp.int32)[None, :]).astype(jnp.int32)
    earlier = jnp.cumsum(one_hot, axis=0) - one_hot
    slot_index = jnp.sum(earlier * one_hot, axis=1)
    destination = flat_ids * capacity + slot_index
    source_row = jnp.full((experts * capacity,), tok_count, jnp.int32)
    source_row = source_row.at[destination].set(
        jnp.arange(pair_count, dtype=jnp.int32) // topk_count
    )
    padded_rows = jnp.concatenate([moe_rows, jnp.zeros((1, width), jnp.bfloat16)], axis=0)
    outgoing = padded_rows[source_row].reshape(experts, capacity, width)
    arrived = lax.all_to_all(outgoing, "dev", split_axis=0, concat_axis=0, tiled=True)
    own_rows = arrived.reshape(experts * capacity, width)
    both_rows = lax.all_gather(own_rows, "role", axis=0, tiled=True)
    expert_sum = lax.psum_scatter(
        expert_block(both_rows, w_gate[0], w_up[0], w_down[0]),
        "role",
        scatter_dimension=0,
        tiled=True,
    )
    finished = expert_sum.astype(jnp.bfloat16).reshape(experts, capacity, width)
    returned = lax.all_to_all(finished, "dev", split_axis=0, concat_axis=0, tiled=True)
    flat_back = returned.reshape(experts * capacity, width)
    picked = flat_back[destination].reshape(tok_count, topk_count, width).astype(jnp.float32)
    moe_out = jnp.sum(picked * gate_weights[:, :, None], axis=1).astype(jnp.bfloat16)
    attended = jax.vmap(attend_row)(q_latent, q_rope, latent_cache, rope_cache, lengths)
    return (moe_out, attended)


def solution(mesh):
    placed = (
        P(("role", "dev"), None),
        P(("role", "dev"), None),
        P(("role", "dev"), None),
        P("dev", None, "role"),
        P("dev", None, "role"),
        P("dev", None, "role"),
        P(("role", "dev"), None, None),
        P(("role", "dev"), None),
        P(("role", "dev"), None, None),
        P(("role", "dev"), None, None),
        P(("role", "dev")),
    )
    return jax.shard_map(
        per_device,
        mesh=mesh,
        in_specs=placed,
        out_specs=(P(("role", "dev"), None), P(("role", "dev"), None, None)),
        check_vma=False,
    )
```

profile of v0, /device:TPU:1, one launch (start us, length us, event | category | flops | bytes accessed | tf_op | source)
XLA Modules:
  0.0 223.4 jit_solution(7646429509567561305)
XLA Ops:
  7.2 0.0 copy-start
  7.2 0.0 all-gather.2.cloned.1.call-start
  7.2 0.8 copy.15
  8.1 0.1 eq.29
  8.2 0.1 eq.25
  8.2 0.7 broadcast_multiply_fusion
  9.0 0.6 reduce-window.6
  9.6 0.2 slice_reduce_fusion
  9.8 0.1 copy.14
  9.9 0.1 mul.42
  10.0 0.1 fusion.21
  10.1 1.4 scatter_custom_fusion
  11.5 1.0 concatenate.3
  12.5 4.2 %gather_fusion = bf16[512,3584]{1,0:T(8,128)(2,1)} fusion(bf16[33,3584]{1,0:T(8,128)(2,1)S(1)} %concatenate.3, s32[1024]{0:T(1024)S(1)} %pad_clamp_fusion.1), kind=kCustom, calls=%fused_computation | custom fusion | bytes 7342080 | tf_op jit(solution)/shard_map/gather | solution.py:66
  16.7 57.5 %all_to_all.10 = bf16[64,8,3584]{2,1,0:T(8,128)(2,1)} all-to-all(bf16[64,8,3584]{2,1,0:T(8,128)(2,1)} %bitcast.49), channel_id=1, replica_groups=mesh['role'=2,'dev'=64] {'dev'}, dimensions={0} | all-to-all | bytes 7340032 | tf_op jit(solution)/shard_map/all_to_all | solution.py:67
  74.2 0.0 all-gather.2.cloned.1.call-update
  74.2 0.0 reduce-scatter.2.cloned.1.call-start
  74.3 19.5 %all-gather.2.cloned.1.call-done = bf16[1024,3584]{1,0:T(8,128)(2,1)} async-done(((bf16[512,3584]{1,0:T(8,128)(2,1)}), bf16[1024,3584]{1,0:T(8,128)(2,1)}) %all-gather.2.cloned.1.call-update) | async-done | bytes 7340048 | tf_op jit(solution)/shard_map/all_gather | solution.py:69
  93.8 7.3 %fusion.4 = f32[1024,512]{1,0:T(8,128)S(1)} fusion(bf16[1024,3584]{1,0:T(8,128)(2,1)} %all-gather.2.cloned.1.call-done, bf16[1,3584,512]{2,1,0:T(8,128)(2,1)} %param.15), kind=kOutput, calls=%fused_computation.8 | convolution fusion | flops 3758096384 | bytes 13107200 | tf_op jit(solution)/shard_map/dot_general | solution.py:11
  101.1 15.5 %fusion.2 = f32[1024,3584]{1,0:T(8,128)} fusion(bf16[1,3584,512]{2,1,0:T(8,128)(2,1)} %param.16, f32[1024,512]{1,0:T(8,128)S(1)} %fusion.4, bf16[1024,3584]{1,0:T(8,128)(2,1)} %all-gather.2.cloned.1.call-done, bf16[1,3584,512]{2,1,0:T(8,128)(2,1)} %param.14), kind=kOutput, calls=%fused_computation.6 | convolution fusion | flops 7519338496 | bytes 31457280 | tf_op jit(solution)/shard_map/dot_general | solution.py:13
  116.6 0.0 reduce-scatter.2.cloned.1.call-update
  116.6 28.2 %reduce-scatter.2.cloned.1.call-done = f32[512,3584]{1,0:T(8,128)} async-done(((f32[1024,3584]{1,0:T(8,128)}), f32[512,3584]{1,0:T(8,128)}) %reduce-scatter.2.cloned.1.call-update) | async-done | bytes 7340048 | tf_op jit(solution)/shard_map/reduce_scatter | solution.py:70
  144.8 5.3 %convert_bitcast_fusion = bf16[64,8,3584]{2,1,0:T(8,128)(2,1)} fusion(f32[512,3584]{1,0:T(8,128)} %reduce-scatter.2.cloned.1.call-done), kind=kLoop, calls=%fused_computation.12 | loop fusion | flops 1835008 | bytes 11010048 | tf_op jit(solution)/shard_map/reshape | solution.py:76
  150.1 0.0 copy-start.3
  150.1 0.0 copy-start.2
  150.1 0.0 copy-start.4
  150.1 0.0 copy-start.1
  150.1 10.7 %all-to-all-start.1 = ((bf16[64,8,3584]{2,1,0:T(8,128)(2,1)}), bf16[64,8,3584]{2,1,0:T(8,128)(2,1)}, u32[]{:S(2)}, u32[]{:S(2)}) async-start(bf16[64,8,3584]{2,1,0:T(8,128)(2,1)} %convert_bitcast_fusion), calls=%async_computation.2 | async-start | bytes 7340032 | tf_op jit(solution)/shard_map/all_to_all | solution.py:77
  160.8 0.0 copy-done.3
  160.8 0.1 copy.18
  160.8 0.0 copy-done.2
  160.8 0.1 reshape.93
  161.0 0.0 copy-done.4
  161.0 0.1 iota_compare_fusion.2
  161.1 0.0 copy-done.1
  161.1 6.0 %fusion.27 = f32[4,64,2048]{2,1,0:T(8,128)S(1)} fusion(bf16[4,64,512]{2,1,0:T(8,128)(2,1)S(1)} %copy-done.1, bf16[4,2048,512]{2,1,0:T(8,128)(2,1)} %param.19), kind=kOutput, calls=%fused_computation.47 | convolution fusion | flops 536870912 | bytes 10747904 | tf_op jit(solution)/shard_map/vmap()/dot_general | solution.py:21
  167.1 0.0 copy-done
  167.1 2.4 %fusion.26 = (f32[4,64]{1,0:T(4,128)S(1)}, f32[4,64,2048]{2,1,0:T(8,128)}) fusion(pred[4,2048]{1,0:T(4,128)(4,1)S(1)} %iota_compare_fusion.2, f32[4,64,2048]{2,1,0:T(8,128)S(1)} %fusion.27, bf16[4,64,64]{2,1,0:T(8,128)(2,1)S(1)} %reshape.93, bf16[4,64,2048]{2,1,0:T(8,128)(2,1)S(1)} %copy-done), kind=kOutput, calls=%fused_computation.46 | convolution fusion | flops 70256640 | bytes 5284864 | tf_op jit(solution)/shard_map/vmap()/sub | solution.py:32
  169.4 6.3 %convolution_convert_fusion = bf16[4,64,512]{2,1,0:T(8,128)(2,1)} fusion(bf16[4,2048,512]{2,1,0:T(8,128)(2,1)} %param.19, f32[4,64,2048]{2,1,0:T(8,128)} %get-tuple-element.3, f32[4,64]{1,0:T(4,128)S(1)} %get-tuple-element.2), kind=kOutput, calls=%fused_computation.21 | convolution fusion | flops 538050560 | bytes 10748928 | tf_op jit(solution)/shard_map/vmap()/dot_general | solution.py:34
  175.8 32.6 %all-to-all-done.1 = bf16[64,8,3584]{2,1,0:T(8,128)(2,1)} async-done(((bf16[64,8,3584]{2,1,0:T(8,128)(2,1)}), bf16[64,8,3584]{2,1,0:T(8,128)(2,1)}, u32[]{:S(2)}, u32[]{:S(2)}) %all-to-all-start.1) | async-done | bytes 3670048 | tf_op jit(solution)/shard_map/all_to_all | solution.py:77
  208.4 6.0 %gather_fusion.1 = bf16[256,3584]{1,0:T(8,128)(2,1)S(1)} fusion(bf16[512,3584]{1,0:T(8,128)(2,1)} %bitcast.9, s32[1024]{0:T(1024)S(1)} %pad_clamp_fusion), kind=kCustom, calls=%fused_computation.1 | custom fusion | bytes 3671040 | tf_op jit(solution)/shard_map/gather | solution.py:79
  214.5 2.1 fusion.1
  (8 shorter events, 0.1 us)
Async XLA Ops:
  7.2 159.9 %copy-start = (bf16[4,64,2048]{2,1,0:T(8,128)(2,1)S(1)}, bf16[4,64,2048]{2,1,0:T(8,128)(2,1)}, u32[]{:S(2)}) copy-start(bf16[4,64,2048]{2,1,0:T(8,128)(2,1)} %param.20) | copy-start | bytes 3145732
  7.2 86.6 %all-gather.2.cloned.1.call-start = ((), (), s32[]{:S(2)}) async-start(), calls=%async_computation.3 | async-start | bytes 11010048 | tf_op jit(solution)/shard_map/all_gather | solution.py:69
  74.2 70.5 %reduce-scatter.2.cloned.1.call-start = ((), (), s32[]{:S(2)}) async-start(), calls=%async_computation.4 | async-start | bytes 22020096 | tf_op jit(solution)/shard_map/reduce_scatter | solution.py:70
  150.1 10.7 %copy-start.3 = (f32[32,8]{0,1:T(8,128)S(1)}, f32[32,8]{0,1:T(8,128)}, u32[]{:S(2)}) copy-start(f32[32,8]{0,1:T(8,128)} %param.13) | copy-start | bytes 3076
  150.1 10.8 %copy-start.2 = (bf16[4,4096]{1,0:T(4,128)(2,1)S(1)}, bf16[4,4096]{1,0:T(4,128)(2,1)}, u32[]{:S(2)}) copy-start(bf16[4,4096]{1,0:T(4,128)(2,1)} %param.18) | copy-start | bytes 98308
  150.1 10.9 %copy-start.4 = (s32[4]{0:T(128)S(1)}, s32[4]{0:T(128)}, u32[]{:S(2)}) copy-start(s32[4]{0:T(128)} %param.21) | copy-start | bytes 52
  150.1 11.0 %copy-start.1 = (bf16[4,64,512]{2,1,0:T(8,128)(2,1)S(1)}, bf16[4,64,512]{2,1,0:T(8,128)(2,1)}, u32[]{:S(2)}) copy-start(bf16[4,64,512]{2,1,0:T(8,128)(2,1)} %param.17) | copy-start | bytes 786436
  150.1 58.3 %all-to-all-start.1 = ((bf16[64,8,3584]{2,1,0:T(8,128)(2,1)}), bf16[64,8,3584]{2,1,0:T(8,128)(2,1)}, u32[]{:S(2)}, u32[]{:S(2)}) async-start(bf16[64,8,3584]{2,1,0:T(8,128)(2,1)} %convert_bitcast_fusion), calls=%async_computation.2 | async-start | bytes 7340032 | tf_op jit(solution)/shard_map/all_to_all | solution.py:77
Sparse Core Ops, SparseCore 0:
  74.4 19.3 all-gather.1
  116.7 28.0 reduce-scatter.1
where the time goes:
time: 224 us; the launch traced here: 223 us
  waiting for transfers between devices  80.4 us (36%)
  blocking collectives  57.5 us (26%)
  matrix products  37.5 us (17%)
  local copies, waits for them, and re-layouts  14.2 us (6%)
  between operations  14.2 us (6%)
  starting transfers between devices  10.8 us (5%)
  other arithmetic  8.97 us (4%)
    all_to_all x1, blocking collectives, per_device(): lax.all_to_all(outgoing, 'dev', split_axis=0, concat_axis=0, tiled=True)  57.5 us
    all_to_all x1, waiting for transfers between devices, per_device(): lax.all_to_all(finished, 'dev', split_axis=0, concat_axis=0, tiled=True)  32.6 us
    reduce_scatter x1, waiting for transfers between devices, per_device(): lax.psum_scatter(expert_block(both_rows, w_gate[0], w_up[0], w_down[0]),...  28.2 us
    all_gather x1, waiting for transfers between devices, per_device(): both_rows = lax.all_gather(own_rows, 'role', axis=0, tiled=True)  19.5 us
    dot_general x1, matrix products, expert_block(): lax.dot_general(hidden_units, down_matrix, (((1,), (1,)), ((), ())), pref...  15.5 us
    all_to_all x1, starting transfers between devices, per_device(): lax.all_to_all(finished, 'dev', split_axis=0, concat_axis=0, tiled=True)  10.7 us
    dot_general x1, matrix products, expert_block(): up_part = jnp.dot(chosen, up_matrix, preferred_element_type=jnp.float32)  7.29 us
    dot_general x1, matrix products, attend_row(): jnp.dot(probs, cache_lat, preferred_element_type=jnp.float32)  6.34 us
  transfers between devices with their start and end apart: 3, of which 3 were waited for; matrix products, arithmetic and copies ran while one was open for 7% of the time, Pallas kernels for 0%

commit v1 on v0

--- a/solution.py
+++ b/solution.py
@@ -4,6 +4,11 @@
 from jax.sharding import PartitionSpec as P
 
 score_scale = 192.0 ** (-0.5)
+
+
+def gather_over(x, axis, dim):
+    sent = jnp.stack([x] * lax.axis_size(axis))
+    return jnp.concatenate(lax.all_to_all(sent, axis, 0, 0), axis=dim)
 
 
 def expert_block(chosen, gate_matrix, up_matrix, down_matrix):
@@ -66,7 +71,7 @@
     outgoing = padded_rows[source_row].reshape(experts, capacity, width)
     arrived = lax.all_to_all(outgoing, "dev", split_axis=0, concat_axis=0, tiled=True)
     own_rows = arrived.reshape(experts * capacity, width)
-    both_rows = lax.all_gather(own_rows, "role", axis=0, tiled=True)
+    both_rows = gather_over(own_rows, "role", 0)
     expert_sum = lax.psum_scatter(
         expert_block(both_rows, w_gate[0], w_up[0], w_down[0]),
         "role",

time: 224 us -> 211 us (0.942)
  waiting for transfers between devices: 80.4 us -> 55.9 us
  blocking collectives: 57.5 us -> 69.3 us
  matrix products: 37.5 us -> 34.1 us
  local copies, waits for them, and re-layouts: 14.2 us -> 17.1 us
    all_gather x1 -> x0, waiting for transfers between devices: 19.5 us -> none  [per_device(): both_rows = lax.all_gather(own_rows, 'role', axis=0, tiled=True)]
    all_to_all x0 -> x1, blocking collectives: none -> 11.9 us  [gather_over(): return jnp.concatenate(lax.all_to_all(sent, axis, 0, 0), axis=dim)]
    reduce_scatter x1, waiting for transfers between devices: 28.2 us -> 23.2 us  [per_device(): lax.psum_scatter(expert_block(both_rows, w_gate[0], w_up[0], w_down[0]),...]
    dot_general x1, matrix products: 7.29 us -> 3.93 us  [expert_block(): up_part = jnp.dot(chosen, up_matrix, preferred_element_type=jnp.float32)]
    unnamed x12 -> x16, local copies, waits for them, and re-layouts: 0.94 us -> 3.89 us
  transfers between devices with their start and end apart: 3 -> 2, of which waited for: 3 -> 2; matrix products, arithmetic and copies ran while one was open for 7% -> 7% of each run, Pallas kernels for 0% -> 0%
where the time goes in v1:
time: 211 us
  blocking collectives  69.3 us (33%)
  waiting for transfers between devices  55.9 us (26%)
  matrix products  34.1 us (16%)
  local copies, waits for them, and re-layouts  17.1 us (8%)
  between operations  14.2 us (7%)
  starting transfers between devices  10.7 us (5%)
  other arithmetic  9.6 us (5%)
    all_to_all x1, blocking collectives, per_device(): lax.all_to_all(outgoing, 'dev', split_axis=0, concat_axis=0, tiled=True)  57.4 us
    all_to_all x1, waiting for transfers between devices, per_device(): lax.all_to_all(finished, 'dev', split_axis=0, concat_axis=0, tiled=True)  32.6 us
    reduce_scatter x1, waiting for transfers between devices, per_device(): lax.psum_scatter(expert_block(both_rows, w_gate[0], w_up[0], w_down[0]),...  23.2 us
    dot_general x1, matrix products, expert_block(): lax.dot_general(hidden_units, down_matrix, (((1,), (1,)), ((), ())), pref...  15.5 us
    all_to_all x1, blocking collectives, gather_over(): return jnp.concatenate(lax.all_to_all(sent, axis, 0, 0), axis=dim)  11.9 us
    all_to_all x1, starting transfers between devices, per_device(): lax.all_to_all(finished, 'dev', split_axis=0, concat_axis=0, tiled=True)  10.7 us
    dot_general x1, matrix products, attend_row(): jnp.dot(probs, cache_lat, preferred_element_type=jnp.float32)  6.34 us
    gather x1, local copies, waits for them, and re-layouts, per_device(): flat_back[destination].reshape(tok_count, topk_count, width)  6.04 us
  transfers between devices with their start and end apart: 2, of which 2 were waited for; matrix products, arithmetic and copies ran while one was open for 7% of the time, Pallas kernels for 0%

profile of v1, /device:TPU:1, one launch (start us, length us, event | category | flops | bytes accessed | tf_op | source)
XLA Modules:
  0.0 210.9 jit_solution(12176131654792828475)
XLA Ops:
  7.2 0.0 copy-start
  7.2 0.0 reduce-scatter.2.cloned.1.call-start
  7.2 0.8 copy.15
  8.1 0.1 eq.29
  8.2 0.1 eq.25
  8.2 0.7 broadcast_multiply_fusion
  9.0 0.6 reduce-window.6
  9.6 0.2 slice_reduce_fusion
  9.8 0.1 copy.14
  9.9 0.1 mul.42
  10.0 0.1 fusion.21
  10.1 1.4 scatter_custom_fusion
  11.5 1.0 concatenate.3
  12.5 4.2 %gather_fusion = bf16[512,3584]{1,0:T(8,128)(2,1)} fusion(bf16[33,3584]{1,0:T(8,128)(2,1)S(1)} %concatenate.3, s32[1024]{0:T(1024)S(1)} %pad_clamp_fusion.1), kind=kCustom, calls=%fused_computation | custom fusion | bytes 7342080 | tf_op jit(solution)/shard_map/gather | solution.py:71
  16.6 57.4 %all_to_all.15 = bf16[64,8,3584]{2,1,0:T(8,128)(2,1)S(1)} all-to-all(bf16[64,8,3584]{2,1,0:T(8,128)(2,1)} %bitcast.50), channel_id=1, replica_groups=mesh['role'=2,'dev'=64] {'dev'}, dimensions={0} | all-to-all | bytes 7340032 | tf_op jit(solution)/shard_map/all_to_all | solution.py:72
  74.1 0.6 pad_maximum_fusion
  74.7 0.0 copy-start.6
  74.7 11.9 %all_to_all.16 = bf16[2,512,3584]{2,1,0:T(8,128)(2,1)S(1)} all-to-all(bf16[2,512,3584]{2,1,0:T(8,128)(2,1)S(1)} %pad_maximum_fusion), channel_id=1, replica_groups=mesh['role'=2,'dev'=64] {'role'}, dimensions={0} | all-to-all | bytes 14680064 | tf_op jit(solution)/shard_map/all_to_all | solution.py:11
  86.6 0.0 copy-start.1
  86.6 2.9 %copy-done.1 = bf16[2,512,3584]{2,1,0:T(8,128)(2,1)} copy-done((bf16[2,512,3584]{2,1,0:T(8,128)(2,1)}, bf16[2,512,3584]{2,1,0:T(8,128)(2,1)S(1)}, u32[]{:S(2)}) %copy-start.1) | copy-done | bytes 7340056
  89.5 0.0 copy-done.6
  89.5 3.9 %fusion.4 = f32[1024,512]{1,0:T(8,128)S(1)} fusion(bf16[1024,3584]{1,0:T(8,128)(2,1)S(1)} %bitcast.52, bf16[1,3584,512]{2,1,0:T(8,128)(2,1)S(1)} %copy-done.6), kind=kOutput, calls=%fused_computation.9 | convolution fusion | flops 3758096384 | bytes 13107200 | tf_op jit(solution)/shard_map/dot_general | solution.py:16
  93.5 15.5 %fusion.2 = f32[1024,3584]{1,0:T(8,128)} fusion(bf16[1,3584,512]{2,1,0:T(8,128)(2,1)} %param.16, f32[1024,512]{1,0:T(8,128)S(1)} %fusion.4, bf16[1024,3584]{1,0:T(8,128)(2,1)} %bitcast.53, bf16[1,3584,512]{2,1,0:T(8,128)(2,1)} %param.14), kind=kOutput, calls=%fused_computation.7 | convolution fusion | flops 7519338496 | bytes 31457280 | tf_op jit(solution)/shard_map/dot_general | solution.py:18
  109.0 0.0 reduce-scatter.2.cloned.1.call-update
  109.0 23.2 %reduce-scatter.2.cloned.1.call-done = f32[512,3584]{1,0:T(8,128)} async-done(((f32[1024,3584]{1,0:T(8,128)}), f32[512,3584]{1,0:T(8,128)}) %reduce-scatter.2.cloned.1.call-update) | async-done | bytes 7340048 | tf_op jit(solution)/shard_map/reduce_scatter | solution.py:75
  132.2 5.3 %convert_bitcast_fusion = bf16[64,8,3584]{2,1,0:T(8,128)(2,1)} fusion(f32[512,3584]{1,0:T(8,128)} %reduce-scatter.2.cloned.1.call-done), kind=kLoop, calls=%fused_computation.13 | loop fusion | flops 1835008 | bytes 11010048 | tf_op jit(solution)/shard_map/reshape | solution.py:81
  137.5 0.0 copy-start.4
  137.5 0.0 copy-start.3
  137.5 0.0 copy-start.5
  137.5 0.0 copy-start.2
  137.5 10.7 %all-to-all-start.2 = ((bf16[64,8,3584]{2,1,0:T(8,128)(2,1)}), bf16[64,8,3584]{2,1,0:T(8,128)(2,1)}, u32[]{:S(2)}, u32[]{:S(2)}) async-start(bf16[64,8,3584]{2,1,0:T(8,128)(2,1)} %convert_bitcast_fusion), calls=%async_computation.3 | async-start | bytes 7340032 | tf_op jit(solution)/shard_map/all_to_all | solution.py:82
  148.2 0.0 copy-done.4
  148.2 0.1 copy.18
  148.3 0.0 copy-done.3
  148.3 0.1 reshape.93
  148.4 0.0 copy-done.5
  148.4 0.1 iota_compare_fusion.2
  148.5 0.0 copy-done.2
  148.5 6.0 %fusion.27 = f32[4,64,2048]{2,1,0:T(8,128)S(1)} fusion(bf16[4,64,512]{2,1,0:T(8,128)(2,1)S(1)} %copy-done.2, bf16[4,2048,512]{2,1,0:T(8,128)(2,1)} %param.19), kind=kOutput, calls=%fused_computation.48 | convolution fusion | flops 536870912 | bytes 10747904 | tf_op jit(solution)/shard_map/vmap()/dot_general | solution.py:26
  154.5 0.0 copy-done
  154.5 2.4 %fusion.26 = (f32[4,64]{1,0:T(4,128)S(1)}, f32[4,64,2048]{2,1,0:T(8,128)}) fusion(pred[4,2048]{1,0:T(4,128)(4,1)S(1)} %iota_compare_fusion.2, f32[4,64,2048]{2,1,0:T(8,128)S(1)} %fusion.27, bf16[4,64,64]{2,1,0:T(8,128)(2,1)S(1)} %reshape.93, bf16[4,64,2048]{2,1,0:T(8,128)(2,1)S(1)} %copy-done), kind=kOutput, calls=%fused_computation.47 | convolution fusion | flops 70256640 | bytes 5284864 | tf_op jit(solution)/shard_map/vmap()/sub | solution.py:37
  156.9 6.3 %convolution_convert_fusion = bf16[4,64,512]{2,1,0:T(8,128)(2,1)} fusion(bf16[4,2048,512]{2,1,0:T(8,128)(2,1)} %param.19, f32[4,64,2048]{2,1,0:T(8,128)} %get-tuple-element.3, f32[4,64]{1,0:T(4,128)S(1)} %get-tuple-element.2), kind=kOutput, calls=%fused_computation.22 | convolution fusion | flops 538050560 | bytes 10748928 | tf_op jit(solution)/shard_map/vmap()/dot_general | solution.py:39
  163.2 32.6 %all-to-all-done.2 = bf16[64,8,3584]{2,1,0:T(8,128)(2,1)} async-done(((bf16[64,8,3584]{2,1,0:T(8,128)(2,1)}), bf16[64,8,3584]{2,1,0:T(8,128)(2,1)}, u32[]{:S(2)}, u32[]{:S(2)}) %all-to-all-start.2) | async-done | bytes 3670048 | tf_op jit(solution)/shard_map/all_to_all | solution.py:82
  195.8 6.0 %gather_fusion.1 = bf16[256,3584]{1,0:T(8,128)(2,1)S(1)} fusion(bf16[512,3584]{1,0:T(8,128)(2,1)} %bitcast.10, s32[1024]{0:T(1024)S(1)} %pad_clamp_fusion), kind=kCustom, calls=%fused_computation.1 | custom fusion | bytes 3671040 | tf_op jit(solution)/shard_map/gather | solution.py:84
  201.9 2.1 %fusion.1 = bf16[32,3584]{1,0:T(8,128)(2,1)} fusion(bf16[256,3584]{1,0:T(8,128)(2,1)S(1)} %gather_fusion.1, f32[32,8]{1,0:T(8,128)S(1)} %copy.18), kind=kLoop, calls=%fused_computation.6 | loop fusion | flops 2637824 | bytes 2065408 | tf_op jit(solution)/shard_map/reduce_sum | solution.py:85
  (8 shorter events, 0.1 us)
Async XLA Ops:
  7.2 147.4 %copy-start = (bf16[4,64,2048]{2,1,0:T(8,128)(2,1)S(1)}, bf16[4,64,2048]{2,1,0:T(8,128)(2,1)}, u32[]{:S(2)}) copy-start(bf16[4,64,2048]{2,1,0:T(8,128)(2,1)} %param.20) | copy-start | bytes 3145732
  7.2 125.0 %reduce-scatter.2.cloned.1.call-start = ((), (), s32[]{:S(2)}) async-start(), calls=%async_computation.4 | async-start | bytes 22020096 | tf_op jit(solution)/shard_map/reduce_scatter | solution.py:75
  74.7 14.9 %copy-start.6 = (bf16[1,3584,512]{2,1,0:T(8,128)(2,1)S(1)}, bf16[1,3584,512]{2,1,0:T(8,128)(2,1)}, u32[]{:S(2)}) copy-start(bf16[1,3584,512]{2,1,0:T(8,128)(2,1)} %param.15) | copy-start | bytes 11010052
  86.6 2.9 %copy-start.1 = (bf16[2,512,3584]{2,1,0:T(8,128)(2,1)}, bf16[2,512,3584]{2,1,0:T(8,128)(2,1)S(1)}, u32[]{:S(2)}) copy-start(bf16[2,512,3584]{2,1,0:T(8,128)(2,1)S(1)} %all_to_all.16) | copy-start | bytes 22020100
  137.5 10.7 %copy-start.4 = (f32[32,8]{0,1:T(8,128)S(1)}, f32[32,8]{0,1:T(8,128)}, u32[]{:S(2)}) copy-start(f32[32,8]{0,1:T(8,128)} %param.13) | copy-start | bytes 3076
  137.5 10.8 %copy-start.3 = (bf16[4,4096]{1,0:T(4,128)(2,1)S(1)}, bf16[4,4096]{1,0:T(4,128)(2,1)}, u32[]{:S(2)}) copy-start(bf16[4,4096]{1,0:T(4,128)(2,1)} %param.18) | copy-start | bytes 98308
  137.5 10.9 %copy-start.5 = (s32[4]{0:T(128)S(1)}, s32[4]{0:T(128)}, u32[]{:S(2)}) copy-start(s32[4]{0:T(128)} %param.21) | copy-start | bytes 52
  137.5 11.0 %copy-start.2 = (bf16[4,64,512]{2,1,0:T(8,128)(2,1)S(1)}, bf16[4,64,512]{2,1,0:T(8,128)(2,1)}, u32[]{:S(2)}) copy-start(bf16[4,64,512]{2,1,0:T(8,128)(2,1)} %param.17) | copy-start | bytes 786436
  137.5 58.3 %all-to-all-start.2 = ((bf16[64,8,3584]{2,1,0:T(8,128)(2,1)}), bf16[64,8,3584]{2,1,0:T(8,128)(2,1)}, u32[]{:S(2)}, u32[]{:S(2)}) async-start(bf16[64,8,3584]{2,1,0:T(8,128)(2,1)} %convert_bitcast_fusion), calls=%async_computation.3 | async-start | bytes 7340032 | tf_op jit(solution)/shard_map/all_to_all | solution.py:82
Sparse Core Ops, SparseCore 0:
  109.1 23.0 reduce-scatter.1
